TPU v7x, 512 devices: a whole 4x4x16 slice. The times are simulated.
512 devices in a mesh: seq: 128 (over z, y, core), tp: 4 (over x).
Axes of the slice: x: 4, y: 4, z: 16, core: 2. Of those that a mesh axis runs over, the one named last changes fastest.
Arguments:
- tokens: bfloat16 [16384, 1024], P('seq'), may hold values from -6 to 6
- norm_gain: float32 [1024], replicated, may hold values from 0.25 to 1.75
- w_qkv: bfloat16 [1024, 3, 1024], P(None, None, 'tp'), may hold values from -1 to 1
- w_out: bfloat16 [1024, 1024], P('tp'), may hold values from -0.1875 to 0.1875
- head_bias: float32 [2, 16], P(None, 'tp'), may hold values from -1.5 to 1.5
- kv_pool: bfloat16 [512, 128, 2, 1024], P('seq', None, None, 'tp'), may hold values from -6 to 6
- key_variate: int32 [512, 128], P('seq'), may hold values from 0 to 7
- page_table: int32 [128, 4], P('seq'), may hold values from 0 to 3, each once within a row
- node_len: int32 [128], P('seq'), may hold values from 1 to 512, 49152 in all
- path_nodes: int32 [16384, 3], P('seq'), may hold values from 0 to 127, all different within a row; in each aligned block of 128 rows (0 to 127, 128 to 255, ...) at most 8 rows name the same one
- query_variate: int32 [16384], P('seq'), may hold values from 0 to 7
Outputs:
- updated: bfloat16 [16384, 1024], P('seq')
Inputs may be any that keep to these rules, and one draw needn't show every extreme that they name: `path_nodes`: each row names three different nodes; the rows of one device name one node at most 8 times, a bound that some block reaches. `page_table`: each row is a permutation. `node_len`: some node holds exactly 512 tokens.
All inputs are finite; a program needn't handle non-finite values. No bound on the sum of `node_len` on one device may be relied on, other than what follows from the above.
Results may differ from a plain program's by a relative error of at most 0.0033.
The roundings to bfloat16 on the way count: a program that leaves them out, or rounds other values in their place, can miss the bound.
Values may be sent and summed in bfloat16 or wider, within the bound.
A program may use at most 64 MiB of HBM per device.

v0:
```python
import jax
import jax.numpy as jnp
from jax import lax
from jax.sharding import PartitionSpec as P

HD = 64


def head_attend(qh, kh, vh, same, bias_same, bias_diff, valid):
    scores = jnp.dot(qh, kh.T, preferred_element_type=jnp.float32) * HD ** (-0.5)
    scores = scores + jnp.where(same, bias_same, bias_diff)
    scores = jnp.where(valid[None, :], scores, -1e30)
    peak = jnp.max(scores, axis=1)
    weights = jnp.exp(scores - peak[:, None])
    total = jnp.sum(weights, axis=1)
    mixed = (
        jnp.dot(weights.astype(jnp.bfloat16), vh, preferred_element_type=jnp.float32)
        / total[:, None]
    )
    mixed = lax.optimization_barrier(mixed.astype(jnp.bfloat16))
    return (mixed, peak, total)


def place_rows(dest, values, variates, owners, slots):
    onehot = (dest[:, None] == jnp.arange(owners, dtype=jnp.int32)[None, :]).astype(jnp.int32)
    before = jnp.cumsum(onehot, axis=0) - onehot
    slot = jnp.sum(before * onehot, axis=1)
    flat = dest * slots + slot
    width = values.shape[1]
    qbuf = (
        jnp.zeros((owners * slots, width), jnp.bfloat16)
        .at[flat]
        .set(values)
        .reshape(owners, slots, width)
    )
    vbuf = jnp.zeros((owners * slots,), jnp.int32).at[flat].set(variates).reshape(owners, slots)
    return (qbuf, vbuf, flat)


def body(
    tokens,
    norm_gain,
    w_qkv,
    w_out,
    head_bias,
    kv_pool,
    key_variate,
    page_table,
    node_len,
    path_nodes,
    query_variate,
):
    tok_rows, width = tokens.shape
    heads_here = w_qkv.shape[2] // HD
    owners = lax.axis_size("seq")
    slots = min(tok_rows, 8 * tok_rows // owners)
    xf = tokens.astype(jnp.float32)
    normed = (xf * lax.rsqrt(jnp.mean(xf * xf, axis=1, keepdims=True) + 1e-05) * norm_gain).astype(
        jnp.bfloat16
    )
    qkv = jnp.dot(
        normed, w_qkv.reshape(width, 3 * heads_here * HD), preferred_element_type=jnp.float32
    ).astype(jnp.bfloat16)
    qkv = qkv.reshape(tok_rows, 3, heads_here, HD)
    query, key, value = (qkv[:, 0], qkv[:, 1], qkv[:, 2])
    order = page_table[0]
    node_slots = kv_pool.shape[0] * kv_pool.shape[1]
    pages = kv_pool[order].reshape(node_slots, 2, heads_here, HD)
    node_keys = jnp.moveaxis(pages[:, 0], 1, 0)
    node_values = jnp.moveaxis(pages[:, 1], 1, 0)
    key_var = key_variate[order].reshape(node_slots)
    valid = jnp.arange(node_slots, dtype=jnp.int32) < node_len[0]
    qflat = query.reshape(tok_rows, heads_here * HD)
    out_list, peak_list, total_list = ([], [], [])
    for level in range(3):
        qbuf, vbuf, flat = place_rows(path_nodes[:, level], qflat, query_variate, owners, slots)
        owner_qbuf = lax.all_to_all(qbuf, "seq", split_axis=0, concat_axis=0, tiled=True)
        owner_vbuf = lax.all_to_all(vbuf, "seq", split_axis=0, concat_axis=0, tiled=True)
        sources, count, cols = owner_qbuf.shape
        rows = sources * count
        heads_q = jnp.moveaxis(owner_qbuf.reshape(rows, heads_here, HD), 1, 0)
        same = owner_vbuf.reshape(rows)[:, None] == key_var[None, :]

        def per_head(xs):
            return head_attend(xs[0], xs[1], xs[2], same, xs[3], xs[4], valid)

        mixed, peak, total = lax.map(
            per_head, (heads_q, node_keys, node_values, head_bias[1], head_bias[0])
        )
        mixed = jnp.moveaxis(mixed, 0, 1).reshape(sources, count, cols)
        peak = peak.T.reshape(sources, count, heads_here)
        total = total.T.reshape(sources, count, heads_here)
        mixed_back = lax.all_to_all(mixed, "seq", split_axis=0, concat_axis=0, tiled=True)
        peak_back = lax.all_to_all(peak, "seq", split_axis=0, concat_axis=0, tiled=True)
        total_back = lax.all_to_all(total, "seq", split_axis=0, concat_axis=0, tiled=True)
        mixed = mixed_back
        peak = peak_back
        total = total_back
        out_list.append(mixed.reshape(owners * slots, -1)[flat].reshape(tok_rows, heads_here, HD))
        peak_list.append(peak.reshape(owners * slots, heads_here)[flat])
        total_list.append(total.reshape(owners * slots, heads_here)[flat])
    outs = jnp.stack(out_list, axis=1)
    peaks = jnp.stack(peak_list, axis=1)
    totals = jnp.stack(total_list, axis=1)
    own_peak = (
        jnp.sum(query.astype(jnp.float32) * key.astype(jnp.float32), axis=2) * HD ** (-0.5)
        + head_bias[1][None, :]
    )
    all_o = jnp.concatenate([value.astype(jnp.float32)[:, None], outs.astype(jnp.float32)], axis=1)
    all_m = jnp.concatenate([own_peak[:, None], peaks], axis=1)
    all_l = jnp.concatenate([jnp.ones((tok_rows, 1, heads_here), jnp.float32), totals], axis=1)
    top = jnp.max(all_m, axis=1, keepdims=True)
    scale = all_l * jnp.exp(all_m - top)
    attn = (jnp.sum(scale[..., None] * all_o, axis=1) / jnp.sum(scale, axis=1)[..., None]).astype(
        jnp.bfloat16
    )
    partial_sum = jnp.dot(
        attn.reshape(tok_rows, heads_here * HD), w_out, preferred_element_type=jnp.float32
    )
    total_sum = lax.psum(partial_sum, "tp")
    return (xf + total_sum).astype(jnp.bfloat16)


def solution(mesh):
    in_specs = (
        P("seq", None),
        P(),
        P(None, None, "tp"),
        P("tp", None),
        P(None, "tp"),
        P("seq", None, None, "tp"),
        P("seq", None),
        P("seq", None),
        P("seq"),
        P("seq", None),
        P("seq"),
    )
    out_specs = P("seq", None)
    return jax.shard_map(body, mesh=mesh, in_specs=in_specs, out_specs=out_specs, check_vma=False)
```

profile of v0, /device:TPU:1, one launch (start us, length us, event | category | flops | bytes accessed | tf_op | source)
XLA Modules:
  0.0 596.6 jit_solution(2339595824714031808)
XLA Ops:
  11.8 20.6 %all-to-all-start.7 = ((s32[128,1,8]{2,1,0:T(1,128)}), s32[128,1,8]{2,1,0:T(1,128)S(1)}, u32[]{:S(2)}, u32[]{:S(2)}) async-start(s32[128,1,8]{2,1,0:T(1,128)} %bitcast.38), calls=%async_computation.7 | async-start | bytes 131072 | tf_op jit(solution)/shard_map/all_to_all | solution.py:78
  37.1 10.2 %all-to-all-done.7 = s32[128,1,8]{2,1,0:T(1,128)S(1)} async-done(((s32[128,1,8]{2,1,0:T(1,128)}), s32[128,1,8]{2,1,0:T(1,128)S(1)}, u32[]{:S(2)}, u32[]{:S(2)}) %all-to-all-start.7) | async-done | bytes 4128 | tf_op jit(solution)/shard_map/all_to_all | solution.py:78
  47.2 5.9 all-to-all-start.4
  55.9 12.1 %all-to-all-done.4 = s32[128,1,8]{2,1,0:T(1,128)S(1)} async-done(((s32[128,1,8]{2,1,0:T(1,128)}), s32[128,1,8]{2,1,0:T(1,128)S(1)}, u32[]{:S(2)}, u32[]{:S(2)}) %all-to-all-start.4) | async-done | bytes 4128 | tf_op jit(solution)/shard_map/all_to_all | solution.py:78
  68.0 5.7 all-to-all-start.1
  76.3 12.4 %all-to-all-done.1 = s32[128,1,8]{2,1,0:T(1,128)S(1)} async-done(((s32[128,1,8]{2,1,0:T(1,128)}), s32[128,1,8]{2,1,0:T(1,128)S(1)}, u32[]{:S(2)}, u32[]{:S(2)}) %all-to-all-start.1) | async-done | bytes 4128 | tf_op jit(solution)/shard_map/all_to_all | solution.py:78
  88.7 6.2 %all-to-all-start.6 = ((bf16[128,8,256]{2,1,0:T(8,128)(2,1)}), bf16[128,8,256]{2,1,0:T(8,128)(2,1)S(1)}, u32[]{:S(2)}, u32[]{:S(2)}) async-start(bf16[128,8,256]{2,1,0:T(8,128)(2,1)} %bitcast.36), calls=%async_computation.6 | async-start | bytes 1048576 | tf_op jit(solution)/shard_map/all_to_all | solution.py:77
  96.8 29.3 %all-to-all-done.6 = bf16[128,8,256]{2,1,0:T(8,128)(2,1)S(1)} async-done(((bf16[128,8,256]{2,1,0:T(8,128)(2,1)}), bf16[128,8,256]{2,1,0:T(8,128)(2,1)S(1)}, u32[]{:S(2)}, u32[]{:S(2)}) %all-to-all-start.6) | async-done | bytes 524320 | tf_op jit(solution)/shard_map/all_to_all | solution.py:77
  126.1 8.8 %all-to-all-start.3 = ((bf16[128,8,256]{2,1,0:T(8,128)(2,1)}), bf16[128,8,256]{2,1,0:T(8,128)(2,1)S(1)}, u32[]{:S(2)}, u32[]{:S(2)}) async-start(bf16[128,8,256]{2,1,0:T(8,128)(2,1)} %bitcast.25), calls=%async_computation.3 | async-start | bytes 1048576 | tf_op jit(solution)/shard_map/all_to_all | solution.py:77
  147.1 18.6 %all-to-all-done.3 = bf16[128,8,256]{2,1,0:T(8,128)(2,1)S(1)} async-done(((bf16[128,8,256]{2,1,0:T(8,128)(2,1)}), bf16[128,8,256]{2,1,0:T(8,128)(2,1)S(1)}, u32[]{:S(2)}, u32[]{:S(2)}) %all-to-all-start.3) | async-done | bytes 524320 | tf_op jit(solution)/shard_map/all_to_all | solution.py:77
  165.7 9.1 %all-to-all-start = ((bf16[128,8,256]{2,1,0:T(8,128)(2,1)}), bf16[128,8,256]{2,1,0:T(8,128)(2,1)S(1)}, u32[]{:S(2)}, u32[]{:S(2)}) async-start(bf16[128,8,256]{2,1,0:T(8,128)(2,1)} %bitcast.6), calls=%async_computation | async-start | bytes 1048576 | tf_op jit(solution)/shard_map/all_to_all | solution.py:77
  174.9 26.5 %while.47 = (s32[]{:T(128)}, bf16[4,1024,64]{1,2,0:T(8,128)(2,1)S(1)}, f32[4,1024]{1,0:T(4,128)S(1)}, f32[4,1024]{1,0:T(4,128)S(1)}, bf16[4,1024,64]{2,1,0:T(8,1...) while((s32[]{:T(128)}, ...), condition=%wide.region_24.25_spmd.clone, body=%wide.region_21.24_spmd.clone.sunk | while | flops 139590144 | bytes 7255225 | solution.py:87
  205.6 14.9 %all-to-all-start.11 = ((f32[128,8,4]{1,2,0:T(4,128)}), f32[128,8,4]{1,2,0:T(4,128)}, u32[]{:S(2)}, u32[]{:S(2)}) async-start(f32[128,8,4]{1,2,0:T(4,128)} %copy.156), calls=%async_computation.11 | async-start | bytes 524288 | tf_op jit(solution)/shard_map/all_to_all | solution.py:94
  220.6 25.9 %while.46 = (s32[]{:T(128)}, bf16[4,1024,64]{1,2,0:T(8,128)(2,1)S(1)}, f32[4,1024]{1,0:T(4,128)S(1)}, f32[4,1024]{1,0:T(4,128)S(1)}, bf16[4,1024,64]{2,1,0:T(8,1...) while((s32[]{:T(128)}, ...), condition=%wide.region_16.17_spmd.clone, body=%wide.region_13.16_spmd.clone.sunk | while | flops 139590144 | bytes 7255225 | solution.py:87
  249.1 16.1 %all-to-all-start.10 = ((f32[128,8,4]{1,2,0:T(4,128)}), f32[128,8,4]{1,2,0:T(4,128)S(1)}, u32[]{:S(2)}, u32[]{:S(2)}) async-start(f32[128,8,4]{1,2,0:T(4,128)} %copy.154), calls=%async_computation.10 | async-start | bytes 524288 | tf_op jit(solution)/shard_map/all_to_all | solution.py:94
  265.3 26.3 %while.45 = (s32[]{:T(128)}, bf16[4,1024,64]{1,2,0:T(8,128)(2,1)S(1)}, f32[4,1024]{1,0:T(4,128)S(1)}, f32[4,1024]{1,0:T(4,128)S(1)}, bf16[4,1024,64]{2,1,0:T(8,1...) while((s32[]{:T(128)}, ...), condition=%wide.region_8.9_spmd.clone, body=%wide.region_5.8_spmd.clone.sunk | while | flops 139590144 | bytes 7255225 | solution.py:87
  280.3 2.8 fusion.104
  292.7 16.1 %all-to-all-start.9 = ((f32[128,8,4]{1,2,0:T(4,128)}), f32[128,8,4]{1,2,0:T(4,128)S(1)}, u32[]{:S(2)}, u32[]{:S(2)}) async-start(f32[128,8,4]{1,2,0:T(4,128)} %copy.152), calls=%async_computation.9 | async-start | bytes 524288 | tf_op jit(solution)/shard_map/all_to_all | solution.py:94
  309.9 19.4 %all-to-all-done.9 = f32[128,8,4]{1,2,0:T(4,128)S(1)} async-done(((f32[128,8,4]{1,2,0:T(4,128)}), f32[128,8,4]{1,2,0:T(4,128)S(1)}, u32[]{:S(2)}, u32[]{:S(2)}) %all-to-all-start.9) | async-done | bytes 16416 | tf_op jit(solution)/shard_map/all_to_all | solution.py:94
  329.3 8.3 %all-to-all-start.8 = ((f32[128,8,4]{1,2,0:T(4,128)}), f32[128,8,4]{1,2,0:T(4,128)S(1)}, u32[]{:S(2)}, u32[]{:S(2)}) async-start(f32[128,8,4]{1,2,0:T(4,128)} %copy.147), calls=%async_computation.8 | async-start | bytes 524288 | tf_op jit(solution)/shard_map/all_to_all | solution.py:95
  338.6 19.4 %all-to-all-done.8 = f32[128,8,4]{1,2,0:T(4,128)S(1)} async-done(((f32[128,8,4]{1,2,0:T(4,128)}), f32[128,8,4]{1,2,0:T(4,128)S(1)}, u32[]{:S(2)}, u32[]{:S(2)}) %all-to-all-start.8) | async-done | bytes 16416 | tf_op jit(solution)/shard_map/all_to_all | solution.py:95
  358.1 8.5 %all-to-all-start.5 = ((f32[128,8,4]{1,2,0:T(4,128)}), f32[128,8,4]{1,2,0:T(4,128)S(1)}, u32[]{:S(2)}, u32[]{:S(2)}) async-start(f32[128,8,4]{1,2,0:T(4,128)} %copy.140), calls=%async_computation.5 | async-start | bytes 524288 | tf_op jit(solution)/shard_map/all_to_all | solution.py:95
  369.3 17.8 %all-to-all-done.5 = f32[128,8,4]{1,2,0:T(4,128)S(1)} async-done(((f32[128,8,4]{1,2,0:T(4,128)}), f32[128,8,4]{1,2,0:T(4,128)S(1)}, u32[]{:S(2)}, u32[]{:S(2)}) %all-to-all-start.5) | async-done | bytes 16416 | tf_op jit(solution)/shard_map/all_to_all | solution.py:95
  387.1 8.8 %all-to-all-start.2 = ((f32[128,8,4]{1,2,0:T(4,128)}), f32[128,8,4]{1,2,0:T(4,128)}, u32[]{:S(2)}, u32[]{:S(2)}) async-start(f32[128,8,4]{1,2,0:T(4,128)} %copy.133), calls=%async_computation.2 | async-start | bytes 524288 | tf_op jit(solution)/shard_map/all_to_all | solution.py:95
  398.1 17.9 %all-to-all-done.2 = f32[128,8,4]{1,2,0:T(4,128)} async-done(((f32[128,8,4]{1,2,0:T(4,128)}), f32[128,8,4]{1,2,0:T(4,128)}, u32[]{:S(2)}, u32[]{:S(2)}) %all-to-all-start.2) | async-done | bytes 16416 | tf_op jit(solution)/shard_map/all_to_all | solution.py:95
  416.0 8.3 %all-to-all-start.14 = ((bf16[128,8,256]{2,1,0:T(8,128)(2,1)}), bf16[128,8,256]{2,1,0:T(8,128)(2,1)S(1)}, u32[]{:S(2)}, u32[]{:S(2)}) async-start(bf16[128,8,256]{2,1,0:T(8,128)(2,1)} %reshape.311), calls=%async_computation.14 | async-start | bytes 1048576 | tf_op jit(solution)/shard_map/all_to_all | solution.py:93
  426.5 28.6 %all-to-all-done.14 = bf16[128,8,256]{2,1,0:T(8,128)(2,1)S(1)} async-done(((bf16[128,8,256]{2,1,0:T(8,128)(2,1)}), bf16[128,8,256]{2,1,0:T(8,128)(2,1)S(1)}, u32[]{:S(2)}, u32[]{:S(2)}) %all-to-all-start.14) | async-done | bytes 524320 | tf_op jit(solution)/shard_map/all_to_all | solution.py:93
  455.1 9.1 %all-to-all-start.13 = ((bf16[128,8,256]{2,1,0:T(8,128)(2,1)}), bf16[128,8,256]{2,1,0:T(8,128)(2,1)S(1)}, u32[]{:S(2)}, u32[]{:S(2)}) async-start(bf16[128,8,256]{2,1,0:T(8,128)(2,1)} %reshape.309), calls=%async_computation.13 | async-start | bytes 1048576 | tf_op jit(solution)/shard_map/all_to_all | solution.py:93
  466.4 28.6 %all-to-all-done.13 = bf16[128,8,256]{2,1,0:T(8,128)(2,1)S(1)} async-done(((bf16[128,8,256]{2,1,0:T(8,128)(2,1)}), bf16[128,8,256]{2,1,0:T(8,128)(2,1)S(1)}, u32[]{:S(2)}, u32[]{:S(2)}) %all-to-all-start.13) | async-done | bytes 524320 | tf_op jit(solution)/shard_map/all_to_all | solution.py:93
  495.0 9.1 %all-to-all-start.12 = ((bf16[128,8,256]{2,1,0:T(8,128)(2,1)}), bf16[128,8,256]{2,1,0:T(8,128)(2,1)S(1)}, u32[]{:S(2)}, u32[]{:S(2)}) async-start(bf16[128,8,256]{2,1,0:T(8,128)(2,1)} %reshape.307), calls=%async_computation.12 | async-start | bytes 1048576 | tf_op jit(solution)/shard_map/all_to_all | solution.py:93
  527.1 7.9 %all-to-all-done.12 = bf16[128,8,256]{2,1,0:T(8,128)(2,1)S(1)} async-done(((bf16[128,8,256]{2,1,0:T(8,128)(2,1)}), bf16[128,8,256]{2,1,0:T(8,128)(2,1)S(1)}, u32[]{:S(2)}, u32[]{:S(2)}) %all-to-all-start.12) | async-done | bytes 524320 | tf_op jit(solution)/shard_map/all_to_all | solution.py:93
  537.3 50.2 %all-reduce.2.cloned.1.call-done = f32[128,1024]{1,0:T(8,128)} async-done(((f32[128,1024]{1,0:T(8,128)}), f32[128,1024]{1,0:T(8,128)}) %all-reduce.2.cloned.1.call-update) | async-done | bytes 524304 | tf_op jit(solution)/shard_map/psum | solution.py:120
  (270 shorter events, 150.6 us)
Async XLA Ops:
  6.5 128.3 %copy-start = (bf16[4,128,2,256]{3,2,1,0:T(2,128)(2,1)S(1)}, bf16[4,128,2,256]{3,2,1,0:T(2,128)(2,1)}, u32[]{:S(2)}) copy-start(bf16[4,128,2,256]{3,2,1,0:T(2,128)(2,1)} %param.22) | copy-start | bytes 1572868
  8.8 44.4 %copy-start.1 = (bf16[128,1024]{1,0:T(8,128)(2,1)S(1)}, bf16[128,1024]{1,0:T(8,128)(2,1)}, u32[]{:S(2)}) copy-start(bf16[128,1024]{1,0:T(8,128)(2,1)} %param.17) | copy-start | bytes 786436
  8.8 44.4 %copy-start.18 = (f32[1024]{0:T(1024)S(1)}, f32[1024]{0:T(1024)}, u32[]{:S(2)}) copy-start(f32[1024]{0:T(1024)} %param.18) | copy-start | bytes 12292
  11.8 35.4 %all-to-all-start.7 = ((s32[128,1,8]{2,1,0:T(1,128)}), s32[128,1,8]{2,1,0:T(1,128)S(1)}, u32[]{:S(2)}, u32[]{:S(2)}) async-start(s32[128,1,8]{2,1,0:T(1,128)} %bitcast.38), calls=%async_computation.7 | async-start | bytes 131072 | tf_op jit(solution)/shard_map/all_to_all | solution.py:78
  47.2 20.8 %all-to-all-start.4 = ((s32[128,1,8]{2,1,0:T(1,128)}), s32[128,1,8]{2,1,0:T(1,128)S(1)}, u32[]{:S(2)}, u32[]{:S(2)}) async-start(s32[128,1,8]{2,1,0:T(1,128)} %bitcast.29), calls=%async_computation.4 | async-start | bytes 131072 | tf_op jit(solution)/shard_map/all_to_all | solution.py:78
  53.9 81.0 %copy-start.20 = (s32[1,4]{1,0:T(1,128)S(1)}, s32[1,4]{1,0:T(1,128)}, u32[]{:S(2)}) copy-start(s32[1,4]{1,0:T(1,128)} %param.24) | copy-start | bytes 52
  54.1 34.7 %copy-start.2 = (bf16[128,768]{0,1:T(8,128)(2,1)}, bf16[128,768]{0,1:T(8,128)(2,1)S(1)}, u32[]{:S(2)}) copy-start(bf16[128,768]{0,1:T(8,128)(2,1)S(1)} %copy.126) | copy-start | bytes 589828
  68.0 20.7 %all-to-all-start.1 = ((s32[128,1,8]{2,1,0:T(1,128)}), s32[128,1,8]{2,1,0:T(1,128)S(1)}, u32[]{:S(2)}, u32[]{:S(2)}) async-start(s32[128,1,8]{2,1,0:T(1,128)} %bitcast.18), calls=%async_computation.1 | async-start | bytes 131072 | tf_op jit(solution)/shard_map/all_to_all | solution.py:78
  88.7 37.3 %all-to-all-start.6 = ((bf16[128,8,256]{2,1,0:T(8,128)(2,1)}), bf16[128,8,256]{2,1,0:T(8,128)(2,1)S(1)}, u32[]{:S(2)}, u32[]{:S(2)}) async-start(bf16[128,8,256]{2,1,0:T(8,128)(2,1)} %bitcast.36), calls=%async_computation.6 | async-start | bytes 1048576 | tf_op jit(solution)/shard_map/all_to_all | solution.py:77
  126.1 39.6 %all-to-all-start.3 = ((bf16[128,8,256]{2,1,0:T(8,128)(2,1)}), bf16[128,8,256]{2,1,0:T(8,128)(2,1)S(1)}, u32[]{:S(2)}, u32[]{:S(2)}) async-start(bf16[128,8,256]{2,1,0:T(8,128)(2,1)} %bitcast.25), calls=%async_computation.3 | async-start | bytes 1048576 | tf_op jit(solution)/shard_map/all_to_all | solution.py:77
  165.7 39.9 %all-to-all-start = ((bf16[128,8,256]{2,1,0:T(8,128)(2,1)}), bf16[128,8,256]{2,1,0:T(8,128)(2,1)S(1)}, u32[]{:S(2)}, u32[]{:S(2)}) async-start(bf16[128,8,256]{2,1,0:T(8,128)(2,1)} %bitcast.6), calls=%async_computation | async-start | bytes 1048576 | tf_op jit(solution)/shard_map/all_to_all | solution.py:77
  205.6 43.5 %all-to-all-start.11 = ((f32[128,8,4]{1,2,0:T(4,128)}), f32[128,8,4]{1,2,0:T(4,128)}, u32[]{:S(2)}, u32[]{:S(2)}) async-start(f32[128,8,4]{1,2,0:T(4,128)} %copy.156), calls=%async_computation.11 | async-start | bytes 524288 | tf_op jit(solution)/shard_map/all_to_all | solution.py:94
  249.1 43.5 %all-to-all-start.10 = ((f32[128,8,4]{1,2,0:T(4,128)}), f32[128,8,4]{1,2,0:T(4,128)S(1)}, u32[]{:S(2)}, u32[]{:S(2)}) async-start(f32[128,8,4]{1,2,0:T(4,128)} %copy.154), calls=%async_computation.10 | async-start | bytes 524288 | tf_op jit(solution)/shard_map/all_to_all | solution.py:94
  291.6 214.0 %copy-start.17 = (f32[4]{0:T(128)}, f32[4]{0:T(128)S(1)}, u32[]{:S(2)}) copy-start(f32[4]{0:T(128)S(1)} %get-tuple-element.898) | copy-start | bytes 52
  292.7 94.4 %copy-start.3 = (f32[128,8,4]{1,2,0:T(4,128)}, f32[128,8,4]{1,2,0:T(4,128)S(1)}, u32[]{:S(2)}) copy-start(f32[128,8,4]{1,2,0:T(4,128)S(1)} %all-to-all-done.10) | copy-start | bytes 49156
  292.7 36.6 %all-to-all-start.9 = ((f32[128,8,4]{1,2,0:T(4,128)}), f32[128,8,4]{1,2,0:T(4,128)S(1)}, u32[]{:S(2)}, u32[]{:S(2)}) async-start(f32[128,8,4]{1,2,0:T(4,128)} %copy.152), calls=%async_computation.9 | async-start | bytes 524288 | tf_op jit(solution)/shard_map/all_to_all | solution.py:94
  329.3 66.6 %copy-start.5 = (f32[128,8,4]{1,2,0:T(4,128)}, f32[128,8,4]{1,2,0:T(4,128)S(1)}, u32[]{:S(2)}) copy-start(f32[128,8,4]{1,2,0:T(4,128)S(1)} %all-to-all-done.9) | copy-start | bytes 49156
  329.3 28.8 %all-to-all-start.8 = ((f32[128,8,4]{1,2,0:T(4,128)}), f32[128,8,4]{1,2,0:T(4,128)S(1)}, u32[]{:S(2)}, u32[]{:S(2)}) async-start(f32[128,8,4]{1,2,0:T(4,128)} %copy.147), calls=%async_computation.8 | async-start | bytes 524288 | tf_op jit(solution)/shard_map/all_to_all | solution.py:95
  358.1 37.8 %copy-start.7 = (f32[128,8,4]{1,2,0:T(4,128)}, f32[128,8,4]{1,2,0:T(4,128)S(1)}, u32[]{:S(2)}) copy-start(f32[128,8,4]{1,2,0:T(4,128)S(1)} %all-to-all-done.8) | copy-start | bytes 49156
  358.1 29.0 %all-to-all-start.5 = ((f32[128,8,4]{1,2,0:T(4,128)}), f32[128,8,4]{1,2,0:T(4,128)S(1)}, u32[]{:S(2)}, u32[]{:S(2)}) async-start(f32[128,8,4]{1,2,0:T(4,128)} %copy.140), calls=%async_computation.5 | async-start | bytes 524288 | tf_op jit(solution)/shard_map/all_to_all | solution.py:95
  387.1 8.8 %copy-start.9 = (f32[128,8,4]{1,2,0:T(4,128)}, f32[128,8,4]{1,2,0:T(4,128)S(1)}, u32[]{:S(2)}) copy-start(f32[128,8,4]{1,2,0:T(4,128)S(1)} %all-to-all-done.5) | copy-start | bytes 49156
  387.1 28.9 %all-to-all-start.2 = ((f32[128,8,4]{1,2,0:T(4,128)}), f32[128,8,4]{1,2,0:T(4,128)}, u32[]{:S(2)}, u32[]{:S(2)}) async-start(f32[128,8,4]{1,2,0:T(4,128)} %copy.133), calls=%async_computation.2 | async-start | bytes 524288 | tf_op jit(solution)/shard_map/all_to_all | solution.py:95
  416.0 39.1 %all-to-all-start.14 = ((bf16[128,8,256]{2,1,0:T(8,128)(2,1)}), bf16[128,8,256]{2,1,0:T(8,128)(2,1)S(1)}, u32[]{:S(2)}, u32[]{:S(2)}) async-start(bf16[128,8,256]{2,1,0:T(8,128)(2,1)} %reshape.311), calls=%async_computation.14 | async-start | bytes 1048576 | tf_op jit(solution)/shard_map/all_to_all | solution.py:93
  455.1 39.9 %all-to-all-start.13 = ((bf16[128,8,256]{2,1,0:T(8,128)(2,1)}), bf16[128,8,256]{2,1,0:T(8,128)(2,1)S(1)}, u32[]{:S(2)}, u32[]{:S(2)}) async-start(bf16[128,8,256]{2,1,0:T(8,128)(2,1)} %reshape.309), calls=%async_computation.13 | async-start | bytes 1048576 | tf_op jit(solution)/shard_map/all_to_all | solution.py:93
  466.4 42.4 %copy-start.4 = (f32[128,8,4]{1,2,0:T(4,128)S(1)}, f32[128,8,4]{1,2,0:T(4,128)}, u32[]{:S(2)}) copy-start(f32[128,8,4]{1,2,0:T(4,128)} %copy-done.3) | copy-start | bytes 49156
  466.4 43.9 %copy-start.6 = (f32[128,8,4]{1,2,0:T(4,128)S(1)}, f32[128,8,4]{1,2,0:T(4,128)}, u32[]{:S(2)}) copy-start(f32[128,8,4]{1,2,0:T(4,128)} %copy-done.5) | copy-start | bytes 49156
  495.0 39.9 %all-to-all-start.12 = ((bf16[128,8,256]{2,1,0:T(8,128)(2,1)}), bf16[128,8,256]{2,1,0:T(8,128)(2,1)S(1)}, u32[]{:S(2)}, u32[]{:S(2)}) async-start(bf16[128,8,256]{2,1,0:T(8,128)(2,1)} %reshape.307), calls=%async_computation.12 | async-start | bytes 1048576 | tf_op jit(solution)/shard_map/all_to_all | solution.py:93
  504.1 83.3 %all-reduce.2.cloned.1.call-start = ((), (), s32[]{:S(2)}) async-start(), calls=%async_computation.15 | async-start | bytes 1048576 | tf_op jit(solution)/shard_map/psum | solution.py:120
  509.6 6.5 %copy-start.8 = (f32[128,8,4]{1,2,0:T(4,128)S(1)}, f32[128,8,4]{1,2,0:T(4,128)}, u32[]{:S(2)}) copy-start(f32[128,8,4]{1,2,0:T(4,128)} %copy-done.7) | copy-start | bytes 49156
  511.2 7.2 %copy-start.10 = (f32[128,8,4]{1,2,0:T(4,128)S(1)}, f32[128,8,4]{1,2,0:T(4,128)}, u32[]{:S(2)}) copy-start(f32[128,8,4]{1,2,0:T(4,128)} %copy-done.9) | copy-start | bytes 49156
  519.2 16.9 %copy-start.12 = (bf16[128,1,4,64]{0,3,2,1:T(8,128)(2,1)S(1)}, bf16[128,1,4,64]{0,3,2,1:T(8,128)(2,1)}, u32[]{:S(2)}) copy-start(bf16[128,1,4,64]{0,3,2,1:T(8,128)(2,1)} %get-tuple-element.507) | copy-start | bytes 196612
  520.8 15.4 %copy-start.11 = (bf16[256,1024]{1,0:T(8,128)(2,1)S(1)}, bf16[256,1024]{1,0:T(8,128)(2,1)}, u32[]{:S(2)}) copy-start(bf16[256,1024]{1,0:T(8,128)(2,1)} %param.20) | copy-start | bytes 1572868
  (5 other events, 21.8 us)
Sparse Core Ops, SparseCore 0:
  537.4 50.0 all-reduce.1
where the time goes:
time: 608 us; the launch traced here: 597 us
  waiting for transfers between devices  274 us (45%)
  starting transfers between devices  155 us (25%)
  local copies, waits for them, and re-layouts  77 us (13%)
  matrix products  51.7 us (9%)
  other arithmetic  23.1 us (4%)
  between operations  14.5 us (2%)
    all_to_all x3, waiting for transfers between devices, body(): lax.all_to_all(mixed, 'seq', split_axis=0, concat_axis=0, tiled=True)  65.2 us
    all_to_all x3, waiting for transfers between devices, body(): lax.all_to_all(total, 'seq', split_axis=0, concat_axis=0, tiled=True)  55.1 us
    psum x1, waiting for transfers between devices, body(): total_sum = lax.psum(partial_sum, 'tp')  50.2 us
    all_to_all x3, waiting for transfers between devices, body(): lax.all_to_all(qbuf, 'seq', split_axis=0, concat_axis=0, tiled=True)  49.5 us
    all_to_all x3, starting transfers between devices, body(): lax.all_to_all(peak, 'seq', split_axis=0, concat_axis=0, tiled=True)  47.1 us
    all_to_all x3, waiting for transfers between devices, body(): lax.all_to_all(vbuf, 'seq', split_axis=0, concat_axis=0, tiled=True)  34.7 us
    dot_general x12, matrix products, head_attend(): jnp.dot(qh, kh.T, preferred_element_type=jnp.float32) * HD ** (-0.5)  33.5 us
    all_to_all x3, starting transfers between devices, body(): lax.all_to_all(vbuf, 'seq', split_axis=0, concat_axis=0, tiled=True)  32.1 us
  transfers between devices with their start and end apart: 16, of which 14 were waited for; matrix products, arithmetic and copies ran while one was open for 24% of the time, Pallas kernels for 0%

commit v1 on v0

v1 whole, which is shorter than its diff:
```python
import functools

import jax
import jax.numpy as jnp
from jax import lax
from jax.experimental import pallas as pl
from jax.experimental.pallas import tpu as pltpu
from jax.sharding import PartitionSpec as P

HD = 64
CAP = 8
MESH = pl.DeviceIdType.MESH
NT = (((1,), (1,)), ((), ()))
F32, BF16, I32 = jnp.float32, jnp.bfloat16, jnp.int32


def iota(shape, axis):
    return lax.broadcasted_iota(I32, shape, axis)


def kernel(
    dims,
    qkv_ref, x_ref, w_ref, bias_ref, k_ref, v_ref, kvar_ref, pt_ref, len_ref, path_ref, qvar_ref,
    out_ref,
    qall, meta, psend, prec, rsend, rrec, ssend, srec, zsend, zrec, zsrec,
    kext, vt, wall, attn, fb, acc_o, acc_s, own_m,
    ring_s, ring_r, meta_s, meta_r, p_s, p_r, r_s, r_r, st_s, st_r, z_s, z_r, zs_s, zs_r,
    w_s, w_r, a_s, a_r, local_s,
):
    NZ, NP, TP = dims
    NS = NZ // 2
    T = x_ref.shape[0]
    cols = k_ref.shape[1]
    heads = cols // HD
    keys = k_ref.shape[0]
    pages, page = kvar_ref.shape
    nodes = NZ * NP
    R = NP * 2 * CAP
    half = NP * CAP

    s = lax.axis_index("seq")
    t = lax.axis_index("tp")
    z = s // NP
    p = s % NP

    def zdev(d):
        return (((z + d) % NZ) * NP + p, t)

    def pdev(d):
        return (z * NP + (p + d) % NP, t)

    def tdev(d):
        return (s, (t + d) % TP)

    barrier = pltpu.get_barrier_semaphore()
    for d in range(1, NZ):
        pl.semaphore_signal(barrier, inc=1, device_id=zdev(d), device_id_type=MESH)
    for d in range(1, NP):
        pl.semaphore_signal(barrier, inc=1, device_id=pdev(d), device_id_type=MESH)
    for d in range(1, TP):
        pl.semaphore_signal(barrier, inc=1, device_id=tdev(d), device_id_type=MESH)

    def rdma(src, dst, ss, rs, dev):
        return pltpu.make_async_remote_copy(
            src_ref=src, dst_ref=dst, send_sem=ss, recv_sem=rs, device_id=dev, device_id_type=MESH
        )

    path = path_ref[...]
    lane_n = iota((T, nodes), 1)
    hit = [path[:, j : j + 1] == lane_n for j in range(3)]
    hits = sum(h.astype(F32) for h in hit).astype(BF16)
    before = (iota((T, T), 0) > iota((T, T), 1)).astype(F32).astype(BF16)
    count = jnp.dot(before, hits, preferred_element_type=F32)
    packed = jnp.zeros((T, 128), F32)
    lane = iota((T, 128), 1)
    for j in range(3):
        slot = jnp.sum(jnp.where(hit[j], count, 0.0), axis=1, keepdims=True)
        flat = path[:, j : j + 1].astype(F32) * CAP + slot
        packed = jnp.where(lane == j, flat, packed)
        fb[j * T : (j + 1) * T, :] = jnp.broadcast_to(flat, (T, 2 * half)).astype(I32)
    rows = packed.T.astype(I32)
    qall[NS - 1, 0] = qkv_ref[:, 0:cols]
    meta[NS - 1, 0] = jnp.concatenate([rows[0:3], qvar_ref[...]], axis=0)

    pl.semaphore_wait(barrier, NZ + NP + TP - 3)

    def ring(k):
        copies = []
        for way in range(2):
            dev = zdev(1 - 2 * way)
            src = (NS - 1, 0) if k == 1 else (k - 2, way)
            if k < NS:
                copies.append(rdma(qall.at[src], qall.at[k - 1, way], ring_s.at[way, k - 1], ring_r.at[way, k - 1], dev))
                copies.append(rdma(meta.at[src], meta.at[k - 1, way], meta_s.at[way, k - 1], meta_r.at[way, k - 1], dev))
            else:
                part = pl.ds(way * (T // 2), T // 2)
                copies.append(
                    rdma(qall.at[src + (part,)], qall.at[NS - 1, 1, part], ring_s.at[way, k - 1], ring_r.at[way, k - 1], dev)
                )
                if way == 0:
                    copies.append(rdma(meta.at[src], meta.at[NS - 1, 1], meta_s.at[0, k - 1], meta_r.at[0, k - 1], dev))
        return copies

    started = []

    def start(copies):
        for c in copies:
            c.start()
        started.extend(copies)
        return copies

    ring_now = start(ring(1))
    w_copies = start([rdma(w_ref, wall.at[t], w_s.at[d - 1], w_r.at[d - 1], tdev(d)) for d in range(1, TP)])
    w_local = pltpu.make_async_copy(w_ref, wall.at[t], local_s)
    w_local.start()

    length = len_ref[0]
    lane_p = iota((1, page), 1)
    var = kvar_ref[...]
    kk = k_ref[...].astype(F32) * HD ** (-0.5)
    head_of_lane = iota((keys, cols), 1) // HD
    sub = iota((128, page), 0)
    for h in range(heads):
        kext[h, :, 0:cols] = jnp.where(head_of_lane == h, kk, 0.0).astype(BF16)
        other, same = bias_ref[0, h], bias_ref[1, h]
        for g in range(pages):
            place = sum(jnp.where(pt_ref[0, i] == g, i, 0) for i in range(pages))
            valid = place * page + lane_p < length
            b = jnp.where(var[g : g + 1] == sub % 8, same, other)
            hi = b.astype(BF16).astype(F32)
            mid = (b - hi).astype(BF16).astype(F32)
            low = b - hi - mid
            piece = jnp.where(sub < 8, jnp.where(valid, hi, -1e30), jnp.where(valid, jnp.where(sub < 16, mid, low), 0.0))
            piece = jnp.where(sub < 24, piece, 0.0)
            kext[h, g * page : (g + 1) * page, cols : cols + 128] = piece.T.astype(BF16)
    vt[...] = v_ref[...].astype(F32).T.astype(BF16)

    prod = qkv_ref[:, 0:cols].astype(F32) * qkv_ref[:, cols : 2 * cols].astype(F32)
    own_m[...] = jnp.concatenate(
        [jnp.sum(prod[:, h * HD : (h + 1) * HD], axis=1, keepdims=True) * HD ** (-0.5) + bias_ref[1, h] for h in range(heads)],
        axis=1,
    )
    acc_o[...] = jnp.zeros_like(acc_o)
    acc_s[...] = jnp.zeros_like(acc_s)

    row = iota((R, 1), 0)
    target = (z * NP + row // (2 * CAP)) * CAP + row % CAP
    which = (row // CAP) % 2
    sub_t = iota((128, T), 0)

    def select(i):
        sel, one = [], []
        for b in range(2):
            m = meta[i, b]
            want = jnp.where(which == b, target, -1)
            got = (m[0:1] == want) | (m[1:2] == want) | (m[2:3] == want)
            sel.append(got.astype(F32).astype(BF16))
            one.append(((m[3:4] == sub_t % 8) & (sub_t < 24)).astype(F32).astype(BF16))
        sel = jnp.concatenate(sel, axis=1)
        one = jnp.concatenate(one, axis=1)
        q = jnp.concatenate([qall[i, 0], qall[i, 1]], axis=0)
        qs = jnp.dot(sel, q, preferred_element_type=F32)
        os = lax.dot_general(sel, one, NT, preferred_element_type=F32)
        psend[i, :, :, :, 0:cols] = qs.reshape(NP, 2, CAP, cols).astype(BF16)
        psend[i, :, :, :, cols : cols + 128] = os.reshape(NP, 2, CAP, 128).astype(BF16)
        prec[i, p] = psend[i, p]
        return start(
            [
                rdma(psend.at[i, (p + d) % NP], prec.at[i, p], p_s.at[i, d - 1], p_r.at[i, d - 1], pdev(d))
                for d in range(1, NP)
            ]
        )

    def attend(i, copies):
        for c in copies:
            c.wait_recv()
        rows_q = prec[i].astype(F32).reshape(R, cols + 128).astype(BF16)
        outs, peaks, totals = [], [], []
        for h in range(heads):
            score = lax.dot_general(kext[h], rows_q, NT, preferred_element_type=F32)
            peak = jnp.max(score, axis=0, keepdims=True)
            weight = jnp.exp(score - peak)
            peaks.append(peak)
            totals.append(jnp.sum(weight, axis=0, keepdims=True))
            outs.append(
                jnp.dot(vt[h * HD : (h + 1) * HD, :], weight.astype(BF16), preferred_element_type=F32)
            )
        out = jnp.concatenate(outs, axis=0).T
        rsend[i] = out.reshape(NP, 2, CAP, cols).astype(BF16)
        ssend[i] = jnp.concatenate(peaks + totals, axis=0)
        rrec[i, p] = rsend[i, p]
        srec[i, p] = ssend[i]
        back = []
        for d in range(1, NP):
            back.append(rdma(rsend.at[i, (p + d) % NP], rrec.at[i, p], r_s.at[i, d - 1], r_r.at[i, d - 1], pdev(d)))
            back.append(rdma(ssend.at[i], srec.at[i, p], st_s.at[i, d - 1], st_r.at[i, d - 1], pdev(d)))
        return start(back)

    lane_r = iota((8, R), 1)

    def give_back(i, copies):
        for c in copies:
            c.wait_recv()
        home = []
        for b in range(2):
            acc = jnp.zeros((8, R), F32)
            for o in range(NP):
                tile = srec[i, o]
                shift = (o * CAP + R - p * 2 * CAP - b * CAP + R) % R
                acc = jnp.where(lane_r // CAP == o, pltpu.roll(tile, shift, 1), acc)
            moved = pltpu.roll(acc, half, 1)
            both = jnp.where(lane_r[0:heads] < half, acc[0:heads], moved[heads : 2 * heads])
            if i == NS - 1 and b == 0:
                zrec[i, 0] = rrec[i, :, 0]
                zsrec[i, 0] = both
                continue
            zsend[i, b] = both
            dev = zdev(NS) if i == NS - 1 else zdev((2 * b - 1) * (i + 1))
            home.append(rdma(rrec.at[i, :, b], zrec.at[i, b], z_s.at[i, b], z_r.at[i, b], dev))
            home.append(rdma(zsend.at[i, b], zsrec.at[i, b], zs_s.at[i, b], zs_r.at[i, b], dev))
        return start(home)

    lane_g = iota((3 * T, 2 * half), 1)
    lane_h = iota((heads, 2 * half), 1)

    def collect(i, copies):
        for c in copies:
            c.wait_recv()
        if i == NS - 1:
            first, second = z, (z + NS) % NZ
        else:
            first, second = (z + i + 1) % NZ, (z + NZ - i - 1) % NZ
        want = jnp.where(lane_g < half, first * half + lane_g, second * half + lane_g - half)
        pick = (fb[...] == want).astype(F32)
        both = zrec[i].astype(F32).reshape(2 * half, cols).astype(BF16)
        acc_o[...] += jnp.dot(pick.astype(BF16), both, preferred_element_type=F32)
        s0, s1 = zsrec[i, 0], zsrec[i, 1]
        m = jnp.where(lane_h < half, s0, pltpu.roll(s1, half, 1))
        l = jnp.where(lane_h < half, pltpu.roll(s0, half, 1), s1)
        stats = jnp.concatenate([m, l], axis=0)
        acc_s[...] += lax.dot_general(
            pick, stats, NT, precision=lax.Precision.HIGHEST, preferred_element_type=F32
        )

    sent, back, home = {}, {}, {}
    for k in range(1, NS + 3):
        if k <= NS:
            for c in ring_now:
                c.wait_recv()
            if k < NS:
                ring_now = start(ring(k + 1))
            sent[k - 1] = select(k - 1)
        if 0 <= k - 2 < NS:
            back[k - 2] = attend(k - 2, sent[k - 2])
        if 0 <= k - 3 < NS:
            home[k - 3] = give_back(k - 3, back[k - 3])
    for i in range(NS):
        collect(i, home[i])

    m0 = own_m[...]
    ms = [acc_s[j * T : (j + 1) * T, 0:heads] for j in range(3)]
    ls = [acc_s[j * T : (j + 1) * T, heads : 2 * heads] for j in range(3)]
    top = jnp.maximum(jnp.maximum(m0, ms[0]), jnp.maximum(ms[1], ms[2]))
    w0 = jnp.exp(m0 - top)
    ws = [jnp.exp(m - top) for m in ms]
    den = w0 + ws[0] * ls[0] + ws[1] * ls[1] + ws[2] * ls[2]

    def wide(c):
        return jnp.concatenate([jnp.broadcast_to(c[:, h : h + 1], (T, HD)) for h in range(heads)], axis=1)

    mixed = wide(w0) * qkv_ref[:, 2 * cols : 3 * cols].astype(F32)
    for j in range(3):
        mixed = mixed + wide(ws[j]) * acc_o[j * T : (j + 1) * T, :]
    mixed = mixed / wide(den)
    attn[t] = mixed.astype(BF16)
    a_copies = start(
        [rdma(attn.at[t], attn.at[t], a_s.at[d - 1], a_r.at[d - 1], tdev(d)) for d in range(1, TP)]
    )
    w_local.wait()
    for c in w_copies:
        c.wait_recv()
    for c in a_copies:
        c.wait_recv()
    total = jnp.zeros(out_ref.shape, F32)
    for j in range(TP):
        total = total + jnp.dot(attn[j], wall[j], preferred_element_type=F32)
    out_ref[...] = (x_ref[...].astype(F32) + total).astype(BF16)
    for c in started:
        c.wait_send()


def body(
    dims,
    tokens,
    norm_gain,
    w_qkv,
    w_out,
    head_bias,
    kv_pool,
    key_variate,
    page_table,
    node_len,
    path_nodes,
    query_variate,
):
    NZ, NP, TP = dims
    NS = NZ // 2
    T, width = tokens.shape
    cols = w_qkv.shape[2]
    heads = cols // HD
    pages, page = key_variate.shape
    keys = pages * page
    R = NP * 2 * CAP
    half = NP * CAP
    xf = tokens.astype(F32)
    normed = (xf * lax.rsqrt(jnp.mean(xf * xf, axis=1, keepdims=True) + 1e-05) * norm_gain).astype(BF16)
    qkv = jnp.dot(normed, w_qkv.reshape(width, 3 * cols), preferred_element_type=F32).astype(BF16)
    k = kv_pool[:, :, 0].reshape(keys, cols)
    v = kv_pool[:, :, 1].reshape(keys, cols)
    vmem = pl.BlockSpec(memory_space=pltpu.VMEM)
    smem = pl.BlockSpec(memory_space=pltpu.SMEM)
    dma = pltpu.SemaphoreType.DMA
    scratch = [
        pltpu.VMEM((NS, 2, T, cols), BF16),
        pltpu.VMEM((NS, 2, 4, T), I32),
        pltpu.VMEM((NS, NP, 2, CAP, cols + 128), BF16),
        pltpu.VMEM((NS, NP, 2, CAP, cols + 128), BF16),
        pltpu.VMEM((NS, NP, 2, CAP, cols), BF16),
        pltpu.VMEM((NS, NP, 2, CAP, cols), BF16),
        pltpu.VMEM((NS, 8, R), F32),
        pltpu.VMEM((NS, NP, 8, R), F32),
        pltpu.VMEM((NS, 2, heads, R), F32),
        pltpu.VMEM((NS, 2, NP, CAP, cols), BF16),
        pltpu.VMEM((NS, 2, heads, R), F32),
        pltpu.VMEM((heads, keys, cols + 128), BF16),
        pltpu.VMEM((cols, keys), BF16),
        pltpu.VMEM((TP,) + w_out.shape, BF16),
        pltpu.VMEM((TP, T, cols), BF16),
        pltpu.VMEM((3 * T, 2 * half), I32),
        pltpu.VMEM((3 * T, cols), F32),
        pltpu.VMEM((3 * T, 2 * heads), F32),
        pltpu.VMEM((T, heads), F32),
    ]
    sems = (
        [dma((2, NS))] * 4 + [dma((NS, NP - 1))] * 6 + [dma((NS, 2))] * 4 + [dma((TP - 1,))] * 4 + [dma(())]
    )
    return pl.pallas_call(
        functools.partial(kernel, dims),
        out_shape=jax.ShapeDtypeStruct((T, width), BF16),
        in_specs=[vmem, vmem, vmem, smem, vmem, vmem, vmem, smem, smem, vmem, vmem],
        out_specs=vmem,
        scratch_shapes=scratch + sems,
        compiler_params=pltpu.CompilerParams(
            collective_id=0, has_side_effects=True, vmem_limit_bytes=56 * 1024 * 1024
        ),
    )(
        qkv, tokens, w_out, head_bias, k, v, key_variate, page_table, node_len, path_nodes,
        query_variate.reshape(1, T),
    )


def build(mesh, plane):
    dims = (mesh.shape["seq"] // plane, plane, mesh.shape["tp"])
    in_specs = (
        P("seq", None),
        P(),
        P(None, None, "tp"),
        P("tp", None),
        P(None, "tp"),
        P("seq", None, None, "tp"),
        P("seq", None),
        P("seq", None),
        P("seq"),
        P("seq", None),
        P("seq"),
    )
    return jax.shard_map(
        functools.partial(body, dims), mesh=mesh, in_specs=in_specs, out_specs=P("seq", None), check_vma=False
    )


def solution(mesh):
    return build(mesh, 8)
```

time: 608 us -> 94.1 us (0.15); the launches traced: 597 us -> 93.1 us
  waiting for transfers between devices: 274 us -> 0 us
  starting transfers between devices: 155 us -> 0 us
  Pallas kernels: 0 us -> 84.6 us
  local copies, waits for them, and re-layouts: 77 us -> 6.37 us
  matrix products: 51.7 us -> 1.36 us
  other arithmetic: 23.1 us -> 0.14 us
  between operations: 14.5 us -> 0.71 us
    all_to_all x15 -> x0, waiting for transfers between devices: 224 us -> none  [the longest x3 65.2 us: body(): lax.all_to_all(mixed, 'seq', split_axis=0, concat_axis=0, tiled=True)]
    all_to_all x15 -> x0, starting transfers between devices: 155 us -> none  [the longest x3 47.1 us: body(): lax.all_to_all(peak, 'seq', split_axis=0, concat_axis=0, tiled=True)]
    pallas_call x0 -> x1, Pallas kernels: none -> 84.6 us  [body(): pl.pallas_call(functools.partial(kernel, dims), out_shape=jax.ShapeDtypeS...]
    dot_general x26 -> x1, matrix products: 51.7 us -> 1.36 us  [body(): jnp.dot(normed, w_qkv.reshape(width, 3 * cols), preferred_element_type=F32)]
    psum x1 -> x0, waiting for transfers between devices: 50.2 us -> none  [body(): total_sum = lax.psum(partial_sum, 'tp')]
    dynamic_slice x24 -> x0, local copies, waits for them, and re-layouts: 14.4 us -> none  [body(): lax.map(per_head, (heads_q, node_keys, node_values, head_bias[1], head_bi...]
    reshape x19 -> x0, local copies, waits for them, and re-layouts: 13.7 us -> none  [the longest x6 4.78 us: body(): total = total.T.reshape(sources, count, heads_here)]
    gather x18 -> x0, local copies, waits for them, and re-layouts: 12.2 us -> none  [the longest x6 3.56 us: body(): peak_list.append(peak.reshape(owners * slots, heads_here)[flat])]
  transfers between devices with their start and end apart: 16 -> 0, of which waited for: 14 -> 0; matrix products, arithmetic and copies ran while one was open for 24% -> 0% of each run, Pallas kernels for 0% -> 0%
where the time goes in v1:
time: 94.1 us; the launch traced here: 93.1 us
  Pallas kernels  84.6 us (90%)
  local copies, waits for them, and re-layouts  6.37 us (7%)
  matrix products  1.36 us (1%)
    pallas_call x1, Pallas kernels, body(): pl.pallas_call(functools.partial(kernel, dims), out_shape=jax.ShapeDtypeS...  84.6 us
    unnamed x13, local copies, waits for them, and re-layouts  5.64 us

profile of v1, /device:TPU:1, one launch (start us, length us, event | category | flops | bytes accessed | tf_op | source)
XLA Modules:
  0.0 93.1 jit_solution(13930458988646759656)
XLA Ops:
  0.0 0.0 copy-start
  0.0 0.0 copy-start.2
  0.0 1.8 %copy.13 = bf16[1024,3,256]{0,2,1:T(8,128)(2,1)S(1)} copy(bf16[1024,3,256]{2,0,1:T(8,128)(2,1)} %param.13) | data formatting | bytes 3145728 | tf_op args[2]
  1.8 0.0 copy-start.1
  1.8 0.0 copy-done
  1.8 0.1 fusion
  1.9 0.0 copy-done.2
  1.9 1.4 %convolution_convert_fusion.qkv_ref = bf16[128,768]{1,0:T(8,128)(2,1)} fusion(bf16[1024,768]{0,1:T(8,128)(2,1)S(1)} %bitcast.5, bf16[128,1024]{1,0:T(8,128)(2,1)S(1)} %copy-done, f32[1024]{0:T(1024)S(1)} %copy-done.2, f32[128]{0:T(128)S(1)} %add_rsqrt_fusion), kind=kOutput, calls=%fused_computation | convolution fusion | flops 201949184 | bytes 2036224 | tf_op jit(solution)/shard_map/dot_general | solution.py:317
  3.3 0.0 copy-done.1
  3.3 0.0 copy-start.3
  3.3 0.7 fusion.6
  4.0 0.7 copy.17
  4.8 0.7 copy.18
  6.2 0.0 copy-done.3
  6.2 0.7 copy.16.path_ref
  6.9 84.6 %shard_map.109 = bf16[128,1024]{1,0:T(8,128)(2,1)} custom-call(bf16[128,768]{1,0:T(8,128)(2,1)} %convolution_convert_fusion.qkv_ref, bf16[128,1024]{1,0:T(8,128)(2,1)} %x_ref.1, bf16[256,1024]{1,0:T(8,128)(2,1)} %w_ref.1, f32[2,4]{1,0:T(2,128)} %bias_ref.1, bf16[512,256]{1,0:T(8,128)(2,1)} %bitcast.6, bf16[512,256]{1,0:T(8,128)(2,1)} %bitcast.7, ...), custom_call_target="tpu_custom_call" | custom-call | tf_op jit(solution)/shard_map/pallas_call | solution.py:347
  91.5 1.7 %copy.21 = bf16[128,1024]{1,0:T(8,128)(2,1)} copy(bf16[128,1024]{1,0:T(8,128)(2,1)} %shard_map.109) | data formatting | bytes 524288
  (1 shorter events, 0.0 us)
Async XLA Ops:
  0.0 1.8 %copy-start = (bf16[128,1024]{1,0:T(8,128)(2,1)S(1)}, bf16[128,1024]{1,0:T(8,128)(2,1)}, u32[]{:S(2)}) copy-start(bf16[128,1024]{1,0:T(8,128)(2,1)} %x_ref.1) | copy-start | bytes 786436
  0.0 1.9 %copy-start.2 = (f32[1024]{0:T(1024)S(1)}, f32[1024]{0:T(1024)}, u32[]{:S(2)}) copy-start(f32[1024]{0:T(1024)} %param.12) | copy-start | bytes 12292
  1.8 1.5 %copy-start.1 = (bf16[4,128,2,256]{3,2,1,0:T(2,128)(2,1)S(1)}, bf16[4,128,2,256]{3,2,1,0:T(2,128)(2,1)}, u32[]{:S(2)}) copy-start(bf16[4,128,2,256]{3,2,1,0:T(2,128)(2,1)} %param.16) | copy-start | bytes 1572868
  3.3 2.9 %copy-start.3 = (s32[128,3]{0,1:T(4,128)S(1)}, s32[128,3]{0,1:T(4,128)}, u32[]{:S(2)}) copy-start(s32[128,3]{0,1:T(4,128)} %param.20) | copy-start | bytes 4612

commit v2 on v1

--- a/solution.py
+++ b/solution.py
@@ -20,19 +20,19 @@
 
 def kernel(
     dims,
-    qkv_ref, x_ref, w_ref, bias_ref, k_ref, v_ref, kvar_ref, pt_ref, len_ref, path_ref, qvar_ref,
+    x_hbm, gain_hbm, wqkv_hbm, w_hbm, bias_hbm, kv_hbm, kvar_hbm, pt_hbm, len_ref, path_hbm, qvar_hbm,
     out_ref,
+    x_ref, gain_ref, wqkv_ref, bias_ref, kv_ref, kvar_ref, pt_ref, path_ref, qvar_ref, qkv,
     qall, meta, psend, prec, rsend, rrec, ssend, srec, zsend, zrec, zsrec,
     kext, vt, wall, attn, fb, acc_o, acc_s, own_m,
     ring_s, ring_r, meta_s, meta_r, p_s, p_r, r_s, r_r, st_s, st_r, z_s, z_r, zs_s, zs_r,
-    w_s, w_r, a_s, a_r, local_s,
+    w_s, w_r, a_s, a_r, local_s, in_s,
 ):
     NZ, NP, TP = dims
     NS = NZ // 2
     T = x_ref.shape[0]
-    cols = k_ref.shape[1]
+    cols = wqkv_ref.shape[2]
     heads = cols // HD
-    keys = k_ref.shape[0]
     pages, page = kvar_ref.shape
     nodes = NZ * NP
     R = NP * 2 * CAP
@@ -53,19 +53,30 @@
         return (s, (t + d) % TP)
 
     barrier = pltpu.get_barrier_semaphore()
-    for d in range(1, NZ):
-        pl.semaphore_signal(barrier, inc=1, device_id=zdev(d), device_id_type=MESH)
-    for d in range(1, NP):
-        pl.semaphore_signal(barrier, inc=1, device_id=pdev(d), device_id_type=MESH)
-    for d in range(1, TP):
-        pl.semaphore_signal(barrier, inc=1, device_id=tdev(d), device_id_type=MESH)
+    friends = [zdev(1), zdev(-1)] + [pdev(d) for d in range(1, NP)] + [tdev(d) for d in range(1, TP)]
+    for dev in friends:
+        pl.semaphore_signal(barrier, inc=1, device_id=dev, device_id_type=MESH)
+
+    loads = {}
+    pairs = dict(
+        path=(path_hbm, path_ref), qvar=(qvar_hbm, qvar_ref), x=(x_hbm, x_ref), gain=(gain_hbm, gain_ref),
+        w0=(wqkv_hbm.at[0], wqkv_ref.at[0]), w1=(wqkv_hbm.at[1], wqkv_ref.at[1]), w2=(wqkv_hbm.at[2], wqkv_ref.at[2]),
+        kv=(kv_hbm, kv_ref), kvar=(kvar_hbm, kvar_ref), bias=(bias_hbm, bias_ref), pt=(pt_hbm, pt_ref),
+        w=(w_hbm, wall.at[t]),
+    )
+    for j, (name, (src, dst)) in enumerate(pairs.items()):
+        loads[name] = pltpu.make_async_copy(src, dst, in_s.at[j])
+        loads[name].start()
 
     def rdma(src, dst, ss, rs, dev):
         return pltpu.make_async_remote_copy(
             src_ref=src, dst_ref=dst, send_sem=ss, recv_sem=rs, device_id=dev, device_id_type=MESH
         )
 
-    path = path_ref[...]
+    loads["path"].wait()
+    loads["qvar"].wait()
+    path_rows = path_ref[...]
+    path = jnp.concatenate([path_rows.astype(F32), jnp.zeros((5, T), F32)], axis=0).T.astype(I32)
     lane_n = iota((T, nodes), 1)
     hit = [path[:, j : j + 1] == lane_n for j in range(3)]
     hits = sum(h.astype(F32) for h in hit).astype(BF16)
@@ -79,26 +90,30 @@
         packed = jnp.where(lane == j, flat, packed)
         fb[j * T : (j + 1) * T, :] = jnp.broadcast_to(flat, (T, 2 * half)).astype(I32)
     rows = packed.T.astype(I32)
-    qall[NS - 1, 0] = qkv_ref[:, 0:cols]
     meta[NS - 1, 0] = jnp.concatenate([rows[0:3], qvar_ref[...]], axis=0)
-
-    pl.semaphore_wait(barrier, NZ + NP + TP - 3)
+    loads["x"].wait()
+    loads["gain"].wait()
+    xf = x_ref[...].astype(F32)
+    normed = (xf * lax.rsqrt(jnp.mean(xf * xf, axis=1, keepdims=True) + 1e-05) * gain_ref[...]).astype(BF16)
+    loads["w0"].wait()
+    qkv[0] = jnp.dot(normed, wqkv_ref[0], preferred_element_type=F32).astype(BF16)
+    qall[NS - 1, 0] = qkv[0]
+
+    pl.semaphore_wait(barrier, len(friends))
 
     def ring(k):
-        copies = []
+        copies = {}
         for way in range(2):
             dev = zdev(1 - 2 * way)
             src = (NS - 1, 0) if k == 1 else (k - 2, way)
-            if k < NS:
-                copies.append(rdma(qall.at[src], qall.at[k - 1, way], ring_s.at[way, k - 1], ring_r.at[way, k - 1], dev))
-                copies.append(rdma(meta.at[src], meta.at[k - 1, way], meta_s.at[way, k - 1], meta_r.at[way, k - 1], dev))
-            else:
-                part = pl.ds(way * (T // 2), T // 2)
-                copies.append(
-                    rdma(qall.at[src + (part,)], qall.at[NS - 1, 1, part], ring_s.at[way, k - 1], ring_r.at[way, k - 1], dev)
-                )
-                if way == 0:
-                    copies.append(rdma(meta.at[src], meta.at[NS - 1, 1], meta_s.at[0, k - 1], meta_r.at[0, k - 1], dev))
+            dst = (k - 1, way) if k < NS else (NS - 1, 1)
+            if k < NS or way == 0:
+                copies[way, "meta"] = rdma(meta.at[src], meta.at[dst], meta_s.at[way, k - 1], meta_r.at[way, k - 1], dev)
+            for c in range(2):
+                part = (pl.ds(c * (T // 2), T // 2),)
+                if k < NS or way == c:
+                    sems = (way, k - 1, c)
+                    copies[way, c] = rdma(qall.at[src + part], qall.at[dst + part], ring_s.at[sems], ring_r.at[sems], dev)
         return copies
 
     started = []
@@ -109,33 +124,40 @@
         started.extend(copies)
         return copies
 
-    ring_now = start(ring(1))
-    w_copies = start([rdma(w_ref, wall.at[t], w_s.at[d - 1], w_r.at[d - 1], tdev(d)) for d in range(1, TP)])
-    w_local = pltpu.make_async_copy(w_ref, wall.at[t], local_s)
-    w_local.start()
+    ring_now = ring(1)
+    start(list(ring_now.values()))
+    w_copies = start([rdma(w_hbm, wall.at[t], w_s.at[d - 1], w_r.at[d - 1], tdev(d)) for d in range(1, TP)])
+    for j in (1, 2):
+        loads["w%d" % j].wait()
+        qkv[j] = jnp.dot(normed, wqkv_ref[j], preferred_element_type=F32).astype(BF16)
+    for name in ("kv", "kvar", "bias", "pt"):
+        loads[name].wait()
 
     length = len_ref[0]
     lane_p = iota((1, page), 1)
     var = kvar_ref[...]
-    kk = k_ref[...].astype(F32) * HD ** (-0.5)
-    head_of_lane = iota((keys, cols), 1) // HD
     sub = iota((128, page), 0)
-    for h in range(heads):
-        kext[h, :, 0:cols] = jnp.where(head_of_lane == h, kk, 0.0).astype(BF16)
-        other, same = bias_ref[0, h], bias_ref[1, h]
-        for g in range(pages):
-            place = sum(jnp.where(pt_ref[0, i] == g, i, 0) for i in range(pages))
-            valid = place * page + lane_p < length
+    even = (iota((page, 2 * page), 1) == 2 * iota((page, 2 * page), 0)).astype(F32).astype(BF16)
+    odd = (iota((page, 2 * page), 1) == 2 * iota((page, 2 * page), 0) + 1).astype(F32).astype(BF16)
+    for g in range(pages):
+        both = kv_ref[g].reshape(2 * page, cols)
+        kk = jnp.dot(even, both, preferred_element_type=F32) * HD ** (-0.5)
+        vt[:, g * page : (g + 1) * page] = jnp.dot(odd, both, preferred_element_type=F32).T.astype(BF16)
+        place = sum(jnp.where(pt_ref[0, i] == g, i, 0) for i in range(pages))
+        valid = place * page + lane_p < length
+        for h in range(heads):
+            other, same = bias_ref[0, h], bias_ref[1, h]
             b = jnp.where(var[g : g + 1] == sub % 8, same, other)
             hi = b.astype(BF16).astype(F32)
             mid = (b - hi).astype(BF16).astype(F32)
             low = b - hi - mid
-            piece = jnp.where(sub < 8, jnp.where(valid, hi, -1e30), jnp.where(valid, jnp.where(sub < 16, mid, low), 0.0))
-            piece = jnp.where(sub < 24, piece, 0.0)
-            kext[h, g * page : (g + 1) * page, cols : cols + 128] = piece.T.astype(BF16)
-    vt[...] = v_ref[...].astype(F32).T.astype(BF16)
-
-    prod = qkv_ref[:, 0:cols].astype(F32) * qkv_ref[:, cols : 2 * cols].astype(F32)
+            piece = jnp.where(sub < 72, jnp.where(valid, hi, -1e30), jnp.where(valid, jnp.where(sub < 80, mid, low), 0.0))
+            piece = jnp.where((sub >= 64) & (sub < 88), piece, 0.0)
+            kext[h, g * page : (g + 1) * page, :] = jnp.concatenate(
+                [kk[:, h * HD : (h + 1) * HD], piece.T[:, HD:]], axis=1
+            ).astype(BF16)
+
+    prod = qkv[0].astype(F32) * qkv[1].astype(F32)
     own_m[...] = jnp.concatenate(
         [jnp.sum(prod[:, h * HD : (h + 1) * HD], axis=1, keepdims=True) * HD ** (-0.5) + bias_ref[1, h] for h in range(heads)],
         axis=1,
@@ -155,7 +177,7 @@
             want = jnp.where(which == b, target, -1)
             got = (m[0:1] == want) | (m[1:2] == want) | (m[2:3] == want)
             sel.append(got.astype(F32).astype(BF16))
-            one.append(((m[3:4] == sub_t % 8) & (sub_t < 24)).astype(F32).astype(BF16))
+            one.append(((m[3:4] == sub_t % 8) & (sub_t >= 64) & (sub_t < 88)).astype(F32).astype(BF16))
         sel = jnp.concatenate(sel, axis=1)
         one = jnp.concatenate(one, axis=1)
         q = jnp.concatenate([qall[i, 0], qall[i, 1]], axis=0)
@@ -171,13 +193,20 @@
             ]
         )
 
+    lane_q = iota((R, 128), 1)
+
     def attend(i, copies):
         for c in copies:
             c.wait_recv()
-        rows_q = prec[i].astype(F32).reshape(R, cols + 128).astype(BF16)
+        rows_q = prec[i].astype(F32).reshape(R, cols + 128)
+        one = rows_q[:, cols : cols + 128]
         outs, peaks, totals = [], [], []
         for h in range(heads):
-            score = lax.dot_general(kext[h], rows_q, NT, preferred_element_type=F32)
+            pair = rows_q[:, h // 2 * 128 : h // 2 * 128 + 128]
+            if h % 2:
+                pair = pltpu.roll(pair, HD, 1)
+            rows_h = jnp.where(lane_q < HD, pair, one).astype(BF16)
+            score = lax.dot_general(kext[h], rows_h, NT, preferred_element_type=F32)
             peak = jnp.max(score, axis=0, keepdims=True)
             weight = jnp.exp(score - peak)
             peaks.append(peak)
@@ -245,10 +274,14 @@
     sent, back, home = {}, {}, {}
     for k in range(1, NS + 3):
         if k <= NS:
-            for c in ring_now:
-                c.wait_recv()
-            if k < NS:
-                ring_now = start(ring(k + 1))
+            ring_next = ring(k + 1) if k < NS else {}
+            for what in ("meta", 0, 1):
+                for way in range(2):
+                    if (way, what) in ring_now:
+                        ring_now[way, what].wait_recv()
+                    if (way, what) in ring_next:
+                        start([ring_next[way, what]])
+            ring_now = ring_next
             sent[k - 1] = select(k - 1)
         if 0 <= k - 2 < NS:
             back[k - 2] = attend(k - 2, sent[k - 2])
@@ -268,7 +301,7 @@
     def wide(c):
         return jnp.concatenate([jnp.broadcast_to(c[:, h : h + 1], (T, HD)) for h in range(heads)], axis=1)
 
-    mixed = wide(w0) * qkv_ref[:, 2 * cols : 3 * cols].astype(F32)
+    mixed = wide(w0) * qkv[2].astype(F32)
     for j in range(3):
         mixed = mixed + wide(ws[j]) * acc_o[j * T : (j + 1) * T, :]
     mixed = mixed / wide(den)
@@ -276,7 +309,7 @@
     a_copies = start(
         [rdma(attn.at[t], attn.at[t], a_s.at[d - 1], a_r.at[d - 1], tdev(d)) for d in range(1, TP)]
     )
-    w_local.wait()
+    loads["w"].wait()
     for c in w_copies:
         c.wait_recv()
     for c in a_copies:
@@ -312,15 +345,20 @@
     keys = pages * page
     R = NP * 2 * CAP
     half = NP * CAP
-    xf = tokens.astype(F32)
-    normed = (xf * lax.rsqrt(jnp.mean(xf * xf, axis=1, keepdims=True) + 1e-05) * norm_gain).astype(BF16)
-    qkv = jnp.dot(normed, w_qkv.reshape(width, 3 * cols), preferred_element_type=F32).astype(BF16)
-    k = kv_pool[:, :, 0].reshape(keys, cols)
-    v = kv_pool[:, :, 1].reshape(keys, cols)
     vmem = pl.BlockSpec(memory_space=pltpu.VMEM)
-    smem = pl.BlockSpec(memory_space=pltpu.SMEM)
+    here = pl.BlockSpec(memory_space=pltpu.HBM)
     dma = pltpu.SemaphoreType.DMA
     scratch = [
+        pltpu.VMEM((T, width), BF16),
+        pltpu.VMEM((1, width), F32),
+        pltpu.VMEM((3, width, cols), BF16),
+        pltpu.SMEM(head_bias.shape, F32),
+        pltpu.VMEM(kv_pool.shape, BF16),
+        pltpu.VMEM((pages, page), I32),
+        pltpu.SMEM(page_table.shape, I32),
+        pltpu.VMEM((3, T), I32),
+        pltpu.VMEM((1, T), I32),
+        pltpu.VMEM((3, T, cols), BF16),
         pltpu.VMEM((NS, 2, T, cols), BF16),
         pltpu.VMEM((NS, 2, 4, T), I32),
         pltpu.VMEM((NS, NP, 2, CAP, cols + 128), BF16),
@@ -332,7 +370,7 @@
         pltpu.VMEM((NS, 2, heads, R), F32),
         pltpu.VMEM((NS, 2, NP, CAP, cols), BF16),
         pltpu.VMEM((NS, 2, heads, R), F32),
-        pltpu.VMEM((heads, keys, cols + 128), BF16),
+        pltpu.VMEM((heads, keys, 128), BF16),
         pltpu.VMEM((cols, keys), BF16),
         pltpu.VMEM((TP,) + w_out.shape, BF16),
         pltpu.VMEM((TP, T, cols), BF16),
@@ -342,21 +380,23 @@
         pltpu.VMEM((T, heads), F32),
     ]
     sems = (
-        [dma((2, NS))] * 4 + [dma((NS, NP - 1))] * 6 + [dma((NS, 2))] * 4 + [dma((TP - 1,))] * 4 + [dma(())]
-    )
-    return pl.pallas_call(
+        [dma((2, NS, 2))] * 2 + [dma((2, NS))] * 2 + [dma((NS, NP - 1))] * 6 + [dma((NS, 2))] * 4 + [dma((TP - 1,))] * 4 + [dma(()), dma((12,))]
+    )
+    call = pl.pallas_call(
         functools.partial(kernel, dims),
         out_shape=jax.ShapeDtypeStruct((T, width), BF16),
-        in_specs=[vmem, vmem, vmem, smem, vmem, vmem, vmem, smem, smem, vmem, vmem],
+        in_specs=[here] * 8 + [pl.BlockSpec(memory_space=pltpu.SMEM)] + [here] * 2,
         out_specs=vmem,
         scratch_shapes=scratch + sems,
         compiler_params=pltpu.CompilerParams(
-            collective_id=0, has_side_effects=True, vmem_limit_bytes=56 * 1024 * 1024
+            collective_id=0, has_side_effects=True, vmem_limit_bytes=40 * 1024 * 1024
         ),
-    )(
-        qkv, tokens, w_out, head_bias, k, v, key_variate, page_table, node_len, path_nodes,
-        query_variate.reshape(1, T),
-    )
+    )
+    operands = (
+        tokens, norm_gain.reshape(1, width), jnp.transpose(w_qkv, (1, 0, 2)), w_out, head_bias, kv_pool, key_variate,
+        page_table, node_len, path_nodes.T, query_variate.reshape(1, T),
+    )
+    return call(*(a if a is node_len else pltpu.with_memory_space_constraint(a, pltpu.HBM) for a in operands))
 
 
 def build(mesh, plane):

time: 94.1 us -> 79 us (0.84)
  Pallas kernels: 84.6 us -> 77.5 us
  local copies, waits for them, and re-layouts: 6.37 us -> 0.71 us
  matrix products: 1.36 us -> 0 us
    pallas_call x1, Pallas kernels: 84.6 us -> 77.5 us  [body(): call(*(a if a is node_len else pltpu.with_memory_space_constraint(a, pltp...]
    unnamed x13 -> x1, local copies, waits for them, and re-layouts: 5.64 us -> 0.71 us
    dot_general x1 -> x0, matrix products: 1.36 us -> none  [body(): jnp.dot(normed, w_qkv.reshape(width, 3 * cols), preferred_element_type=F32)]
where the time goes in v2:
time: 79 us; the launch traced here: 78.8 us
  Pallas kernels  77.5 us (98%)
    pallas_call x1, Pallas kernels, body(): call(*(a if a is node_len else pltpu.with_memory_space_constraint(a, pltp...  77.5 us

profile of v2, /device:TPU:1, one launch (start us, length us, event | category | flops | bytes accessed | tf_op | source)
XLA Modules:
  0.0 78.8 jit_solution(14006492211805233069)
XLA Ops:
  0.7 77.5 %shard_map.109 = bf16[128,1024]{1,0:T(8,128)(2,1)S(1)} custom-call(bf16[128,1024]{1,0:T(8,128)(2,1)} %x_hbm.1, f32[1,1024]{1,0:T(1,128)} %bitcast.5, bf16[3,1024,256]{2,1,0:T(8,128)(2,1)} %bitcast.4, bf16[256,1024]{1,0:T(8,128)(2,1)} %w_hbm.1, f32[2,4]{1,0:T(2,128)} %bias_hbm.1, bf16[4,128,2,256]{3,2,1,0:T(2,128)(2,1)} %kv_hbm.1, s32[4,128]{1,0:T(4,128)} %kvar_hbm.1, ...), custom_call_target="tpu_custom_call" | custom-call | tf_op jit(solution)/shard_map/pallas_call | solution.py:399
  78.1 0.7 copy.14
